TPU v7x, 32 devices: a whole 2x2x4 slice. The times are simulated.
32 devices in a mesh: dp: 16 (over z, y, x), mp: 2 (over core).
Axes of the slice: x: 2, y: 2, z: 4, core: 2. Of those that a mesh axis runs over, the one named last changes fastest.
Arguments:
- residual: bfloat16 [256, 4608], P(None, 'dp'), may hold values from -60 to 60
- norm_gain: float32 [4608], P('dp'), may hold values from 0.25 to 1.75
- query_weight: bfloat16 [4608, 2048], P('dp', 'mp'), may hold values from -2 to 2
- key_weight: bfloat16 [4608, 1024], P('dp', 'mp'), may hold values from -2 to 2
- value_weight: bfloat16 [4608, 1024], P('dp', 'mp'), may hold values from -0.09375 to 0.09375
- out_weight: bfloat16 [2048, 4608], P('mp', 'dp'), may hold values from -1 to 1
- post_gain: float32 [4608], P('dp'), may hold values from 0.25 to 1.75
- encoder_weight: bfloat16 [4608, 8192], P(None, ('dp', 'mp')), may hold values from -0.09375 to 0.09375
- encoder_bias: float32 [8192], P(('dp', 'mp')), may hold values from -3 to 3
- decoder_weight: bfloat16 [8192, 4608], P(('dp', 'mp')), may hold values from -0.125 to 0.125
- decoder_bias: float32 [4608], replicated, may hold values from -3 to 3
Outputs:
- encoder_grad: bfloat16 [4608, 8192], P(None, ('dp', 'mp'))
- encoder_bias_grad: float32 [8192], P(('dp', 'mp'))
- decoder_grad: bfloat16 [8192, 4608], P(('dp', 'mp'))
All inputs are finite; a program needn't handle non-finite values.
Results may differ from a plain program's by a relative error of at most 0.015.
Values may be sent and summed in bfloat16 or wider, within the bound.
No kernel may reach another device: no remote copies, remote signals or barrier semaphores. Data moves between devices by JAX's collectives and lax.ppermute only.
A program may use at most 128 MiB of HBM per device.

v0:
```python
import jax
import jax.numpy as jnp
from jax import lax
from jax.sharding import PartitionSpec as P

HEAD_DIM = 128
epsilon = 1e-06
softcap = 50.0
query_scale = 1.0 / 12.0
rope_base = 10000.0
smoothing = 0.1
penalty = 1.0
loss_weight = 0.0625


def rotate(matrix, positions):
    half_dim = matrix.shape[-1] // 2
    frequency = rope_base ** (-2.0 * jnp.arange(half_dim, dtype=jnp.float32) / matrix.shape[-1])
    angles = positions.astype(jnp.float32)[:, None] * frequency[None, :]
    cosine = jnp.cos(angles)[:, None, :]
    sine_part = jnp.sin(angles)[:, None, :]
    front_half = matrix[..., :half_dim]
    back_half = matrix[..., half_dim:]
    return jnp.concatenate(
        [front_half * cosine - back_half * sine_part, back_half * cosine + front_half * sine_part],
        axis=-1,
    )


def project(summed, square_sum, positions, model_width, query_width, key_width, head_dim):
    inverse = lax.rsqrt(square_sum / model_width + epsilon)
    scaled = summed * inverse[:, None]
    row_count = scaled.shape[0]
    queries = rotate(scaled[:, :query_width].reshape(row_count, -1, head_dim), positions).astype(
        jnp.bfloat16
    )
    keys = rotate(
        scaled[:, query_width : query_width + key_width].reshape(row_count, -1, head_dim), positions
    ).astype(jnp.bfloat16)
    values = (
        scaled[:, query_width + key_width :].reshape(row_count, -1, head_dim).astype(jnp.bfloat16)
    )
    return (queries, keys, values)


def partial_attention(queries, keys, values, query_positions, key_positions):
    row_count, query_heads, head_dim = queries.shape
    key_heads = keys.shape[1]
    grouped = queries.reshape(row_count, key_heads, query_heads // key_heads, head_dim)
    scores = (
        jnp.einsum("rkgd,skd->kgrs", grouped, keys, preferred_element_type=jnp.float32)
        * query_scale
    )
    capped = softcap * jnp.tanh(scores / softcap)
    allowed = query_positions[:, None] >= key_positions[None, :]
    weights = jnp.where(allowed, jnp.exp(capped), 0.0)
    denominator = jnp.sum(weights, axis=3)
    numerator = jnp.einsum(
        "kgrs,skd->rkgd", weights.astype(jnp.bfloat16), values, preferred_element_type=jnp.float32
    )
    return (
        numerator.reshape(row_count, query_heads, head_dim),
        jnp.transpose(denominator, (2, 0, 1)).reshape(row_count, query_heads),
    )


def on_device(
    residual,
    norm_gain,
    query_weight,
    key_weight,
    value_weight,
    out_weight,
    post_gain,
    encoder_weight,
    encoder_bias,
    decoder_weight,
    decoder_bias,
):
    token_count = residual.shape[0]
    model_width = decoder_weight.shape[1]
    head_dim = HEAD_DIM
    query_width = query_weight.shape[1]
    key_width = key_weight.shape[1]
    residual_float = residual.astype(jnp.float32)
    scaled = (residual_float * norm_gain).astype(jnp.bfloat16)
    stacked = jnp.concatenate([query_weight, key_weight, value_weight], axis=1)
    projected_part = jnp.dot(scaled, stacked, preferred_element_type=jnp.float32)
    partial_squares = jnp.sum(residual_float * residual_float, axis=1)
    summed, square_sum = lax.psum((projected_part, partial_squares), "dp")
    positions = jnp.arange(token_count)
    queries, keys, values = project(
        summed, square_sum, positions, model_width, query_width, key_width, head_dim
    )
    numerator, denominator = partial_attention(queries, keys, values, positions, positions)
    attended = (
        (numerator / denominator[:, :, None]).astype(jnp.bfloat16).reshape(token_count, query_width)
    )
    heads_part = jnp.dot(attended, out_weight, preferred_element_type=jnp.float32)
    head_out = lax.psum(heads_part, "mp")
    out_squares = lax.psum(jnp.sum(head_out * head_out, axis=1), "dp")
    normed = head_out * lax.rsqrt(out_squares / model_width + epsilon)[:, None] * post_gain
    hidden_columns = (residual_float + normed).astype(jnp.bfloat16)
    portion = lax.all_gather(hidden_columns, "dp", axis=1, tiled=True)
    preact_sum = jnp.dot(portion, encoder_weight, preferred_element_type=jnp.float32)
    preact_sum, hidden = (preact_sum, portion)
    preact = preact_sum + encoder_bias
    active = smoothing * jax.nn.softplus(preact / smoothing)
    active_low = active.astype(jnp.bfloat16)
    gate_slope = jax.nn.sigmoid(preact / smoothing)
    decoder_norms = jnp.sqrt(
        jnp.sum(jnp.square(decoder_weight.astype(jnp.float32)), axis=1) + epsilon
    )
    activity = jnp.sum(active, axis=0)
    rebuilt_part = jnp.dot(active_low, decoder_weight, preferred_element_type=jnp.float32)
    rebuilt = lax.psum(rebuilt_part, ("dp", "mp"))
    error_low = (rebuilt + decoder_bias - hidden.astype(jnp.float32)).astype(jnp.bfloat16)
    feedback = lax.dot_general(
        error_low, decoder_weight, (((1,), (1,)), ((), ())), preferred_element_type=jnp.float32
    )
    outer_sum = lax.dot_general(
        active_low, error_low, (((0,), (0,)), ((), ())), preferred_element_type=jnp.float32
    )
    grad_active = loss_weight * (2.0 * feedback + penalty * decoder_norms)
    grad_preact = grad_active * gate_slope
    encoder_grad = lax.dot_general(
        hidden,
        grad_preact.astype(jnp.bfloat16),
        (((0,), (0,)), ((), ())),
        preferred_element_type=jnp.float32,
    ).astype(jnp.bfloat16)
    encoder_bias_grad = jnp.sum(grad_preact, axis=0)
    decoder_grad = (
        loss_weight
        * (
            2.0 * outer_sum
            + penalty * (activity / decoder_norms)[:, None] * decoder_weight.astype(jnp.float32)
        )
    ).astype(jnp.bfloat16)
    return (encoder_grad, encoder_bias_grad, decoder_grad)


def solution(mesh):
    placed = (
        P(None, "dp"),
        P("dp"),
        P("dp", "mp"),
        P("dp", "mp"),
        P("dp", "mp"),
        P("mp", "dp"),
        P("dp"),
        P(None, ("dp", "mp")),
        P(("dp", "mp")),
        P(("dp", "mp"), None),
        P(),
    )
    return jax.shard_map(
        on_device,
        mesh=mesh,
        in_specs=placed,
        out_specs=(P(None, ("dp", "mp")), P(("dp", "mp")), P(("dp", "mp"), None)),
        check_vma=False,
    )
```

profile of v0, /device:TPU:0, one launch (start us, length us, event | category | flops | bytes accessed | tf_op | source)
XLA Modules:
  0.0 448.3 jit_solution(4388165543059884381)
XLA Ops:
  7.2 3.6 fusion.4
  11.0 44.4 %psum.36 = f32[256]{0:T(256)S(1)} all-reduce(f32[256]{0:T(256)S(1)} %fusion.21), channel_id=1, replica_groups=mesh['dp'=16,'mp'=2] {'dp'}, use_global_device_ids=true, to_apply=%region_2.0 | all-reduce | flops 256 | bytes 2048 | tf_op jit(solution)/shard_map/psum | solution.py:90
  56.1 1.3 multiply_cosine_fusion
  57.4 85.9 %all-reduce.4.cloned.1.call-done = f32[256,2048]{1,0:T(8,128)} async-done(((f32[256,2048]{1,0:T(8,128)}), f32[256,2048]{1,0:T(8,128)}) %all-reduce.4.cloned.1.call-update) | async-done | bytes 2097168 | tf_op jit(solution)/shard_map/psum | solution.py:90
  143.2 1.8 broadcast_multiply_fusion
  145.1 1.0 slice_bitcast_fusion
  147.1 1.1 fusion.36
  150.8 1.8 copy.25
  152.6 1.1 subtract_convert_fusion.2
  153.7 3.3 fusion.37
  157.0 1.6 fusion.15
  158.7 1.0 fusion.39
  159.8 17.8 %all-reduce.6.cloned.1.call-done = f32[256,288]{0,1:T(8,128)} async-done(((f32[256,288]{0,1:T(8,128)}), f32[256,288]{0,1:T(8,128)}) %all-reduce.6.cloned.1.call-update) | async-done | bytes 294928 | tf_op jit(solution)/shard_map/psum | solution.py:100
  178.6 42.0 %psum.38 = f32[256]{0:T(256)S(1)} all-reduce(f32[256]{0:T(256)S(1)} %multiply_reduce_fusion), channel_id=1, replica_groups=mesh['dp'=16,'mp'=2] {'dp'}, use_global_device_ids=true, to_apply=%region_6.7 | all-reduce | flops 256 | bytes 2048 | tf_op jit(solution)/shard_map/psum | solution.py:101
  220.6 1.7 fusion.22
  222.6 58.1 %all-gather.2.cloned.1.call-done = bf16[256,4608]{0,1:T(8,128)(2,1)} async-done(((bf16[256,288]{0,1:T(8,128)(2,1)}), bf16[256,4608]{0,1:T(8,128)(2,1)}) %all-gather.2.cloned.1.call-update) | async-done | bytes 2359312 | tf_op jit(solution)/shard_map/all_gather | solution.py:104
  280.7 2.8 fusion.29
  283.5 3.3 fusion.34
  286.8 2.2 fusion.3
  289.0 141.6 %all-reduce.8.cloned.1.call-done = f32[256,4608]{0,1:T(8,128)} async-done(((f32[256,4608]{0,1:T(8,128)}), f32[256,4608]{0,1:T(8,128)}) %all-reduce.8.cloned.1.call-update) | async-done | bytes 4718608 | tf_op jit(solution)/shard_map/psum | solution.py:116
  430.6 4.2 subtract_convert_fusion
  434.9 3.1 fusion.2
  438.0 1.4 fusion.38
  439.6 2.2 convolution_convert_fusion
  (53 shorter events, 6.1 us)
Async XLA Ops:
  7.2 273.5 %copy-start = (bf16[4608,256]{1,0:T(8,128)(2,1)S(1)}, bf16[4608,256]{1,0:T(8,128)(2,1)}, u32[]{:S(2)}) copy-start(bf16[4608,256]{1,0:T(8,128)(2,1)} %param.18) | copy-start | bytes 7077892
  7.2 3.8 copy-start.6
  7.2 136.0 %all-reduce.4.cloned.1.call-start = ((), (), s32[]{:S(2)}) async-start(), calls=%async_computation | async-start | bytes 4194304 | tf_op jit(solution)/shard_map/psum | solution.py:90
  10.9 166.7 %all-reduce.6.cloned.1.call-start = ((), (), s32[]{:S(2)}) async-start(), calls=%async_computation.1 | async-start | bytes 589824 | tf_op jit(solution)/shard_map/psum | solution.py:100
  147.1 1.2 copy-start.4
  147.1 1.4 copy-start.7
  147.1 1.4 copy-start.8
  148.5 4.1 copy-start.5
  153.7 3.3 copy-start.9
  157.0 1.7 copy-start.10
  158.6 62.0 %copy-start.12 = (f32[288]{0:T(512)S(1)}, f32[288]{0:T(512)}, u32[]{:S(2)}) copy-start(f32[288]{0:T(512)} %param.17) | copy-start | bytes 3460
  158.6 122.1 %copy-start.13 = (f32[256]{0:T(256)S(1)}, f32[256]{0:T(256)}, u32[]{:S(2)}) copy-start(f32[256]{0:T(256)} %param.19) | copy-start | bytes 3076
  159.8 120.9 %all-gather.2.cloned.1.call-start = ((), (), s32[]{:S(2)}) async-start(), calls=%async_computation.2 | async-start | bytes 2506752 | tf_op jit(solution)/shard_map/all_gather | solution.py:104
  222.4 208.3 %all-reduce.8.cloned.1.call-start = ((), (), s32[]{:S(2)}) async-start(), calls=%async_computation.3 | async-start | bytes 9437184 | tf_op jit(solution)/shard_map/psum | solution.py:116
  280.7 2.8 copy-start.2
  286.8 143.8 %copy-start.11 = (f32[4608]{0:T(1024)S(1)}, f32[4608]{0:T(1024)}, u32[]{:S(2)}) copy-start(f32[4608]{0:T(1024)} %param.21) | copy-start | bytes 55300
  430.6 4.3 copy-start.3
  438.0 1.7 copy-start.1
Sparse Core Ops, SparseCore 0:
  14.1 129.1 all-reduce.3
  159.9 17.6 all-reduce.5
  222.5 58.1 all-gather.1
  287.1 143.4 all-reduce.7
where the time goes:
time: 449 us; the launch traced here: 448 us
  waiting for transfers between devices  303 us (67%)
  blocking collectives  86.3 us (19%)
  matrix products  22.3 us (5%)
  other arithmetic  14.7 us (3%)
  between operations  14 us (3%)
  local copies, waits for them, and re-layouts  7.29 us (2%)
    psum x1, waiting for transfers between devices, on_device(): rebuilt = lax.psum(rebuilt_part, ('dp', 'mp'))  142 us
    psum x1, waiting for transfers between devices, on_device(): summed, square_sum = lax.psum((projected_part, partial_squares), 'dp')  85.9 us
    all_gather x1, waiting for transfers between devices, on_device(): portion = lax.all_gather(hidden_columns, 'dp', axis=1, tiled=True)  58.1 us
    psum x1, blocking collectives, on_device(): summed, square_sum = lax.psum((projected_part, partial_squares), 'dp')  44.4 us
    psum x1, blocking collectives, on_device(): out_squares = lax.psum(jnp.sum(head_out * head_out, axis=1), 'dp')  42 us
    psum x1, waiting for transfers between devices, on_device(): head_out = lax.psum(heads_part, 'mp')  17.8 us
  transfers between devices with their start and end apart: 4, of which 4 were waited for; matrix products, arithmetic and copies ran while one was open for 1% of the time, Pallas kernels for 0%

commit v1 on v0

--- a/solution.py
+++ b/solution.py
@@ -101,7 +101,21 @@
     out_squares = lax.psum(jnp.sum(head_out * head_out, axis=1), "dp")
     normed = head_out * lax.rsqrt(out_squares / model_width + epsilon)[:, None] * post_gain
     hidden_columns = (residual_float + normed).astype(jnp.bfloat16)
-    portion = lax.all_gather(hidden_columns, "dp", axis=1, tiled=True)
+    ways, here, turn = (lax.axis_size("dp"), lax.axis_index("dp"), hidden_columns.shape[1])
+    shape = [n * ways if d == 1 else n for d, n in enumerate(hidden_columns.shape)]
+    full = lax.dynamic_update_slice_in_dim(
+        jnp.zeros(shape, hidden_columns.dtype), hidden_columns, here * turn, axis=1
+    )
+    going_up = going_down = hidden_columns
+    for far in range(1, ways // 2 + 1):
+        going_up = lax.ppermute(going_up, "dp", [(d, (d + 1) % ways) for d in range(ways)])
+        full = lax.dynamic_update_slice_in_dim(full, going_up, (here - far) % ways * turn, axis=1)
+        if 2 * far < ways:
+            going_down = lax.ppermute(going_down, "dp", [(d, (d - 1) % ways) for d in range(ways)])
+            full = lax.dynamic_update_slice_in_dim(
+                full, going_down, (here + far) % ways * turn, axis=1
+            )
+    portion = full
     preact_sum = jnp.dot(portion, encoder_weight, preferred_element_type=jnp.float32)
     preact_sum, hidden = (preact_sum, portion)
     preact = preact_sum + encoder_bias

time: 449 us -> 519 us (1.16)
  local copies, waits for them, and re-layouts: 7.29 us -> 69.1 us
  starting transfers between devices: 0.34 us -> 39.7 us
  waiting for transfers between devices: 303 us -> 271 us
    all_gather x1 -> x0, waiting for transfers between devices: 58.1 us -> none  [on_device(): portion = lax.all_gather(hidden_columns, 'dp', axis=1, tiled=True)]
    dynamic_update_slice x0 -> x16, local copies, waits for them, and re-layouts: none -> 55.8 us  [the longest x8 27.6 us: on_device(): lax.dynamic_update_slice_in_dim(full, going_up, (here - far) % ways * tur...]
    ppermute x0 -> x15, starting transfers between devices: none -> 39.6 us  [the longest x7 39.5 us: on_device(): lax.ppermute(going_down, 'dp', [(d, (d - 1) % ways) for d in range(ways)])]
    ppermute x0 -> x15, waiting for transfers between devices: none -> 23.7 us  [the longest x8 23.6 us: on_device(): lax.ppermute(going_up, 'dp', [(d, (d + 1) % ways) for d in range(ways)])]
  transfers between devices with their start and end apart: 4 -> 18, of which waited for: 4 -> 10; matrix products, arithmetic and copies ran while one was open for 1% -> 12% of each run, Pallas kernels for 0% -> 0%
where the time goes in v1:
time: 519 us; the launch traced here: 516 us
  waiting for transfers between devices  271 us (52%)
  blocking collectives  86.5 us (17%)
  local copies, waits for them, and re-layouts  69.1 us (13%)
  starting transfers between devices  39.7 us (8%)
  matrix products  21.7 us (4%)
  between operations  14.5 us (3%)
  other arithmetic  13.5 us (3%)
    psum x1, waiting for transfers between devices, on_device(): rebuilt = lax.psum(rebuilt_part, ('dp', 'mp'))  144 us
    psum x1, waiting for transfers between devices, on_device(): summed, square_sum = lax.psum((projected_part, partial_squares), 'dp')  85.9 us
    psum x1, blocking collectives, on_device(): summed, square_sum = lax.psum((projected_part, partial_squares), 'dp')  44.4 us
    psum x1, blocking collectives, on_device(): out_squares = lax.psum(jnp.sum(head_out * head_out, axis=1), 'dp')  42.1 us
    ppermute x7, starting transfers between devices, on_device(): lax.ppermute(going_down, 'dp', [(d, (d - 1) % ways) for d in range(ways)])  39.5 us
    dynamic_update_slice x8, local copies, waits for them, and re-layouts, on_device(): lax.dynamic_update_slice_in_dim(full, going_up, (here - far) % ways * tur...  27.6 us
    dynamic_update_slice x7, local copies, waits for them, and re-layouts, on_device(): lax.dynamic_update_slice_in_dim(full, going_down, (here + far) % ways * t...  25 us
    ppermute x8, waiting for transfers between devices, on_device(): lax.ppermute(going_up, 'dp', [(d, (d + 1) % ways) for d in range(ways)])  23.6 us
  transfers between devices with their start and end apart: 18, of which 10 were waited for; matrix products, arithmetic and copies ran while one was open for 12% of the time, Pallas kernels for 0%

profile of v1, /device:TPU:0, one launch (start us, length us, event | category | flops | bytes accessed | tf_op | source)
XLA Modules:
  0.0 516.5 jit_solution(10015215001062204689)
XLA Ops:
  7.2 3.6 fusion.4
  11.0 44.4 %psum.36 = f32[256]{0:T(256)S(1)} all-reduce(f32[256]{0:T(256)S(1)} %fusion.21), channel_id=1, replica_groups=mesh['dp'=16,'mp'=2] {'dp'}, use_global_device_ids=true, to_apply=%region_2.0 | all-reduce | flops 256 | bytes 2048 | tf_op jit(solution)/shard_map/psum | solution.py:90
  57.3 85.9 %all-reduce.4.cloned.1.call-done = f32[256,2048]{1,0:T(8,128)} async-done(((f32[256,2048]{1,0:T(8,128)}), f32[256,2048]{1,0:T(8,128)}) %all-reduce.4.cloned.1.call-update) | async-done | bytes 2097168 | tf_op jit(solution)/shard_map/psum | solution.py:90
  159.8 17.8 %all-reduce.6.cloned.1.call-done = f32[256,288]{0,1:T(8,128)} async-done(((f32[256,288]{0,1:T(8,128)}), f32[256,288]{0,1:T(8,128)}) %all-reduce.6.cloned.1.call-update) | async-done | bytes 294928 | tf_op jit(solution)/shard_map/psum | solution.py:100
  178.6 42.1 %psum.38 = f32[256]{0:T(256)S(1)} all-reduce(f32[256]{0:T(256)S(1)} %multiply_reduce_fusion), channel_id=1, replica_groups=mesh['dp'=16,'mp'=2] {'dp'}, use_global_device_ids=true, to_apply=%region_6.7 | all-reduce | flops 256 | bytes 2048 | tf_op jit(solution)/shard_map/psum | solution.py:101
  221.8 5.6 %collective-permute-start.1 = (bf16[256,288]{0,1:T(8,128)(2,1)S(1)}, bf16[256,288]{0,1:T(8,128)(2,1)S(1)}, u32[]{:S(2)}, u32[]{:S(2)}) collective-permute-start(bf16[256,288]{0,1:T(8,128)(2,1)S(1)} %fusion.22), channel_id=1, source_target_pairs={{0,30},{2,0},{4,2},{6,4},{8,6},{10,8},{12,10},{14,12},{16,14},{18,... | collective-permute-start | bytes 442376 | tf_op jit(solution)/shard_map/ppermute | solution.py:114
  227.5 4.4 collective-permute-done
  231.9 5.6 %collective-permute-start.3 = (bf16[256,288]{0,1:T(8,128)(2,1)S(1)}, bf16[256,288]{0,1:T(8,128)(2,1)S(1)}, u32[]{:S(2)}, u32[]{:S(2)}) collective-permute-start(bf16[256,288]{0,1:T(8,128)(2,1)S(1)} %collective-permute-done.1), channel_id=1, source_target_pairs={{0,30},{2,0},{4,2},{6,4},{8,6},{10,8},{12,10},{14,12},{16,14},{18,... | collective-permute-start | bytes 442376 | tf_op jit(solution)/shard_map/ppermute | solution.py:114
  241.1 5.6 %collective-permute-start.5 = (bf16[256,288]{0,1:T(8,128)(2,1)S(1)}, bf16[256,288]{0,1:T(8,128)(2,1)S(1)}, u32[]{:S(2)}, u32[]{:S(2)}) collective-permute-start(bf16[256,288]{0,1:T(8,128)(2,1)S(1)} %collective-permute-done.3), channel_id=1, source_target_pairs={{0,30},{2,0},{4,2},{6,4},{8,6},{10,8},{12,10},{14,12},{16,14},{18,... | collective-permute-start | bytes 442376 | tf_op jit(solution)/shard_map/ppermute | solution.py:114
  250.0 5.6 %collective-permute-start.7 = (bf16[256,288]{0,1:T(8,128)(2,1)S(1)}, bf16[256,288]{0,1:T(8,128)(2,1)S(1)}, u32[]{:S(2)}, u32[]{:S(2)}) collective-permute-start(bf16[256,288]{0,1:T(8,128)(2,1)S(1)} %collective-permute-done.5), channel_id=1, source_target_pairs={{0,30},{2,0},{4,2},{6,4},{8,6},{10,8},{12,10},{14,12},{16,14},{18,... | collective-permute-start | bytes 442376 | tf_op jit(solution)/shard_map/ppermute | solution.py:114
  258.7 5.7 %collective-permute-start.9 = (bf16[256,288]{0,1:T(8,128)(2,1)S(1)}, bf16[256,288]{0,1:T(8,128)(2,1)S(1)}, u32[]{:S(2)}, u32[]{:S(2)}) collective-permute-start(bf16[256,288]{0,1:T(8,128)(2,1)S(1)} %collective-permute-done.7), channel_id=1, source_target_pairs={{0,30},{2,0},{4,2},{6,4},{8,6},{10,8},{12,10},{14,12},{16,14},{18,... | collective-permute-start | bytes 442376 | tf_op jit(solution)/shard_map/ppermute | solution.py:114
  267.5 5.6 %collective-permute-start.11 = (bf16[256,288]{0,1:T(8,128)(2,1)S(1)}, bf16[256,288]{0,1:T(8,128)(2,1)S(1)}, u32[]{:S(2)}, u32[]{:S(2)}) collective-permute-start(bf16[256,288]{0,1:T(8,128)(2,1)S(1)} %collective-permute-done.9), channel_id=1, source_target_pairs={{0,30},{2,0},{4,2},{6,4},{8,6},{10,8},{12,10},{14,12},{16,14},{18,... | collective-permute-start | bytes 442376 | tf_op jit(solution)/shard_map/ppermute | solution.py:114
  276.3 5.7 %collective-permute-start.13 = (bf16[256,288]{0,1:T(8,128)(2,1)S(1)}, bf16[256,288]{0,1:T(8,128)(2,1)}, u32[]{:S(2)}, u32[]{:S(2)}) collective-permute-start(bf16[256,288]{0,1:T(8,128)(2,1)S(1)} %collective-permute-done.11), channel_id=1, source_target_pairs={{0,30},{2,0},{4,2},{6,4},{8,6},{10,8},{12,10},{14,12},{16,14},{18,... | collective-permute-start | bytes 442376 | tf_op jit(solution)/shard_map/ppermute | solution.py:114
  293.8 3.6 dynamic_update_slice.50
  301.4 3.6 dynamic_update_slice.52
  305.2 3.6 dynamic_update_slice.53
  309.0 3.6 dynamic_update_slice.54
  319.8 3.6 dynamic_update_slice.57
  323.5 3.6 dynamic_update_slice.58
  331.1 3.6 dynamic_update_slice.60
  334.8 3.6 dynamic_update_slice.61
  339.5 3.6 dynamic_update_slice.62
  355.5 144.0 %all-reduce.8.cloned.1.call-done = f32[256,4608]{1,0:T(8,128)} async-done(((f32[256,4608]{1,0:T(8,128)}), f32[256,4608]{1,0:T(8,128)}) %all-reduce.8.cloned.1.call-update) | async-done | bytes 4718608 | tf_op jit(solution)/shard_map/psum | solution.py:130
  499.6 3.8 subtract_convert_fusion
  (145 shorter events, 83.9 us)
Async XLA Ops:
  7.2 340.3 %copy-start = (bf16[4608,256]{1,0:T(8,128)(2,1)S(1)}, bf16[4608,256]{1,0:T(8,128)(2,1)}, u32[]{:S(2)}) copy-start(bf16[4608,256]{1,0:T(8,128)(2,1)} %param.18) | copy-start | bytes 7077892
  7.2 136.0 %all-reduce.4.cloned.1.call-start = ((), (), s32[]{:S(2)}) async-start(), calls=%async_computation | async-start | bytes 4194304 | tf_op jit(solution)/shard_map/psum | solution.py:90
  10.9 166.7 %all-reduce.6.cloned.1.call-start = ((), (), s32[]{:S(2)}) async-start(), calls=%async_computation.1 | async-start | bytes 589824 | tf_op jit(solution)/shard_map/psum | solution.py:100
  158.6 62.1 %copy-start.28 = (f32[288]{0:T(512)S(1)}, f32[288]{0:T(512)}, u32[]{:S(2)}) copy-start(f32[288]{0:T(512)} %param.17) | copy-start | bytes 3460
  159.8 339.8 %all-reduce.8.cloned.1.call-start = ((), (), s32[]{:S(2)}) async-start(), calls=%async_computation.2 | async-start | bytes 9437184 | tf_op jit(solution)/shard_map/psum | solution.py:130
  221.8 10.1 %collective-permute-start = (bf16[256,288]{0,1:T(8,128)(2,1)S(1)}, bf16[256,288]{0,1:T(8,128)(2,1)S(1)}, u32[]{:S(2)}, u32[]{:S(2)}) collective-permute-start(bf16[256,288]{0,1:T(8,128)(2,1)S(1)} %fusion.22), channel_id=1, source_target_pairs={{0,2},{2,4},{4,6},{6,8},{8,10},{10,12},{12,14},{14,16},{16,18},{18... | collective-permute-start | bytes 442376 | tf_op jit(solution)/shard_map/ppermute | solution.py:111
  221.8 10.1 %collective-permute-start.1 = (bf16[256,288]{0,1:T(8,128)(2,1)S(1)}, bf16[256,288]{0,1:T(8,128)(2,1)S(1)}, u32[]{:S(2)}, u32[]{:S(2)}) collective-permute-start(bf16[256,288]{0,1:T(8,128)(2,1)S(1)} %fusion.22), channel_id=1, source_target_pairs={{0,30},{2,0},{4,2},{6,4},{8,6},{10,8},{12,10},{14,12},{16,14},{18,... | collective-permute-start | bytes 442376 | tf_op jit(solution)/shard_map/ppermute | solution.py:114
  231.9 9.2 %collective-permute-start.2 = (bf16[256,288]{0,1:T(8,128)(2,1)S(1)}, bf16[256,288]{0,1:T(8,128)(2,1)S(1)}, u32[]{:S(2)}, u32[]{:S(2)}) collective-permute-start(bf16[256,288]{0,1:T(8,128)(2,1)S(1)} %collective-permute-done), channel_id=1, source_target_pairs={{0,2},{2,4},{4,6},{6,8},{8,10},{10,12},{12,14},{14,16},{16,18},{18... | collective-permute-start | bytes 442376 | tf_op jit(solution)/shard_map/ppermute | solution.py:111
  231.9 9.2 %collective-permute-start.3 = (bf16[256,288]{0,1:T(8,128)(2,1)S(1)}, bf16[256,288]{0,1:T(8,128)(2,1)S(1)}, u32[]{:S(2)}, u32[]{:S(2)}) collective-permute-start(bf16[256,288]{0,1:T(8,128)(2,1)S(1)} %collective-permute-done.1), channel_id=1, source_target_pairs={{0,30},{2,0},{4,2},{6,4},{8,6},{10,8},{12,10},{14,12},{16,14},{18,... | collective-permute-start | bytes 442376 | tf_op jit(solution)/shard_map/ppermute | solution.py:114
  241.1 8.8 %collective-permute-start.4 = (bf16[256,288]{0,1:T(8,128)(2,1)S(1)}, bf16[256,288]{0,1:T(8,128)(2,1)S(1)}, u32[]{:S(2)}, u32[]{:S(2)}) collective-permute-start(bf16[256,288]{0,1:T(8,128)(2,1)S(1)} %collective-permute-done.2), channel_id=1, source_target_pairs={{0,2},{2,4},{4,6},{6,8},{8,10},{10,12},{12,14},{14,16},{16,18},{18... | collective-permute-start | bytes 442376 | tf_op jit(solution)/shard_map/ppermute | solution.py:111
  241.1 32.1 %copy-start.11 = (bf16[256,288]{0,1:T(8,128)(2,1)}, bf16[256,288]{0,1:T(8,128)(2,1)S(1)}, u32[]{:S(2)}) copy-start(bf16[256,288]{0,1:T(8,128)(2,1)S(1)} %collective-permute-done.3) | copy-start | bytes 442372
  241.1 8.8 %collective-permute-start.5 = (bf16[256,288]{0,1:T(8,128)(2,1)S(1)}, bf16[256,288]{0,1:T(8,128)(2,1)S(1)}, u32[]{:S(2)}, u32[]{:S(2)}) collective-permute-start(bf16[256,288]{0,1:T(8,128)(2,1)S(1)} %collective-permute-done.3), channel_id=1, source_target_pairs={{0,30},{2,0},{4,2},{6,4},{8,6},{10,8},{12,10},{14,12},{16,14},{18,... | collective-permute-start | bytes 442376 | tf_op jit(solution)/shard_map/ppermute | solution.py:114
  249.9 8.7 %collective-permute-start.6 = (bf16[256,288]{0,1:T(8,128)(2,1)S(1)}, bf16[256,288]{0,1:T(8,128)(2,1)S(1)}, u32[]{:S(2)}, u32[]{:S(2)}) collective-permute-start(bf16[256,288]{0,1:T(8,128)(2,1)S(1)} %collective-permute-done.4), channel_id=1, source_target_pairs={{0,2},{2,4},{4,6},{6,8},{8,10},{10,12},{12,14},{14,16},{16,18},{18... | collective-permute-start | bytes 442376 | tf_op jit(solution)/shard_map/ppermute | solution.py:111
  249.9 35.1 %copy-start.15 = (bf16[256,288]{0,1:T(8,128)(2,1)}, bf16[256,288]{0,1:T(8,128)(2,1)S(1)}, u32[]{:S(2)}) copy-start(bf16[256,288]{0,1:T(8,128)(2,1)S(1)} %collective-permute-done.5) | copy-start | bytes 442372
  250.0 8.7 %collective-permute-start.7 = (bf16[256,288]{0,1:T(8,128)(2,1)S(1)}, bf16[256,288]{0,1:T(8,128)(2,1)S(1)}, u32[]{:S(2)}, u32[]{:S(2)}) collective-permute-start(bf16[256,288]{0,1:T(8,128)(2,1)S(1)} %collective-permute-done.5), channel_id=1, source_target_pairs={{0,30},{2,0},{4,2},{6,4},{8,6},{10,8},{12,10},{14,12},{16,14},{18,... | collective-permute-start | bytes 442376 | tf_op jit(solution)/shard_map/ppermute | solution.py:114
  258.7 8.8 %collective-permute-start.8 = (bf16[256,288]{0,1:T(8,128)(2,1)S(1)}, bf16[256,288]{0,1:T(8,128)(2,1)S(1)}, u32[]{:S(2)}, u32[]{:S(2)}) collective-permute-start(bf16[256,288]{0,1:T(8,128)(2,1)S(1)} %collective-permute-done.6), channel_id=1, source_target_pairs={{0,2},{2,4},{4,6},{6,8},{8,10},{10,12},{12,14},{14,16},{16,18},{18... | collective-permute-start | bytes 442376 | tf_op jit(solution)/shard_map/ppermute | solution.py:111
  258.7 8.8 %collective-permute-start.9 = (bf16[256,288]{0,1:T(8,128)(2,1)S(1)}, bf16[256,288]{0,1:T(8,128)(2,1)S(1)}, u32[]{:S(2)}, u32[]{:S(2)}) collective-permute-start(bf16[256,288]{0,1:T(8,128)(2,1)S(1)} %collective-permute-done.7), channel_id=1, source_target_pairs={{0,30},{2,0},{4,2},{6,4},{8,6},{10,8},{12,10},{14,12},{16,14},{18,... | collective-permute-start | bytes 442376 | tf_op jit(solution)/shard_map/ppermute | solution.py:114
  267.5 8.8 %collective-permute-start.10 = (bf16[256,288]{0,1:T(8,128)(2,1)S(1)}, bf16[256,288]{0,1:T(8,128)(2,1)S(1)}, u32[]{:S(2)}, u32[]{:S(2)}) collective-permute-start(bf16[256,288]{0,1:T(8,128)(2,1)S(1)} %collective-permute-done.8), channel_id=1, source_target_pairs={{0,2},{2,4},{4,6},{6,8},{8,10},{10,12},{12,14},{14,16},{16,18},{18... | collective-permute-start | bytes 442376 | tf_op jit(solution)/shard_map/ppermute | solution.py:111
  267.5 8.8 %collective-permute-start.11 = (bf16[256,288]{0,1:T(8,128)(2,1)S(1)}, bf16[256,288]{0,1:T(8,128)(2,1)S(1)}, u32[]{:S(2)}, u32[]{:S(2)}) collective-permute-start(bf16[256,288]{0,1:T(8,128)(2,1)S(1)} %collective-permute-done.9), channel_id=1, source_target_pairs={{0,30},{2,0},{4,2},{6,4},{8,6},{10,8},{12,10},{14,12},{16,14},{18,... | collective-permute-start | bytes 442376 | tf_op jit(solution)/shard_map/ppermute | solution.py:114
  276.3 8.7 %collective-permute-start.12 = (bf16[256,288]{0,1:T(8,128)(2,1)S(1)}, bf16[256,288]{0,1:T(8,128)(2,1)S(1)}, u32[]{:S(2)}, u32[]{:S(2)}) collective-permute-start(bf16[256,288]{0,1:T(8,128)(2,1)S(1)} %collective-permute-done.10), channel_id=1, source_target_pairs={{0,2},{2,4},{4,6},{6,8},{8,10},{10,12},{12,14},{14,16},{16,18},{18... | collective-permute-start | bytes 442376 | tf_op jit(solution)/shard_map/ppermute | solution.py:111
  276.3 62.1 %collective-permute-start.13 = (bf16[256,288]{0,1:T(8,128)(2,1)S(1)}, bf16[256,288]{0,1:T(8,128)(2,1)}, u32[]{:S(2)}, u32[]{:S(2)}) collective-permute-start(bf16[256,288]{0,1:T(8,128)(2,1)S(1)} %collective-permute-done.11), channel_id=1, source_target_pairs={{0,30},{2,0},{4,2},{6,4},{8,6},{10,8},{12,10},{14,12},{16,14},{18,... | collective-permute-start | bytes 442376 | tf_op jit(solution)/shard_map/ppermute | solution.py:114
  285.1 58.0 %collective-permute-start.14 = (bf16[256,288]{0,1:T(8,128)(2,1)S(1)}, bf16[256,288]{0,1:T(8,128)(2,1)}, u32[]{:S(2)}, u32[]{:S(2)}) collective-permute-start(bf16[256,288]{0,1:T(8,128)(2,1)S(1)} %collective-permute-done.12), channel_id=1, source_target_pairs={{0,2},{2,4},{4,6},{6,8},{8,10},{10,12},{12,14},{14,16},{16,18},{18... | collective-permute-start | bytes 442376 | tf_op jit(solution)/shard_map/ppermute | solution.py:111
  319.7 27.7 %copy-start.29 = (f32[256]{0:T(256)S(1)}, f32[256]{0:T(256)}, u32[]{:S(2)}) copy-start(f32[256]{0:T(256)} %param.19) | copy-start | bytes 3076
  353.3 146.3 %copy-start.27 = (f32[4608]{0:T(1024)S(1)}, f32[4608]{0:T(1024)}, u32[]{:S(2)}) copy-start(f32[4608]{0:T(1024)} %param.21) | copy-start | bytes 55300
  (24 other events, 257.4 us)
Sparse Core Ops, SparseCore 0:
  14.1 129.1 all-reduce.3
  159.9 17.6 all-reduce.5
  353.4 146.1 all-reduce.7
